TPU v7x, 32 devices: a whole 2x2x4 slice. The times are simulated.
32 devices in a mesh: dp: 4 (over x, core), group: 8 (over z, y).
Axes of the slice: x: 2, y: 2, z: 4, core: 2. Of those that a mesh axis runs over, the one named last changes fastest.
Arguments:
- features: bfloat16 [8192, 3072], P(('dp', 'group')), may hold values from -6 to 6
- target_embed: bfloat16 [8192, 256], P(('dp', 'group')), may hold values from -80 to 80
- proj_weight: bfloat16 [3072, 256], replicated, may hold values from -0.109375 to 0.109375
- prototypes: float32 [2048, 256], replicated, may hold values from -20 to 20
Outputs:
- grad_feat: bfloat16 [8192, 3072], P(('dp', 'group'))
- grad_proj: float32 [3072, 256], P('group')
- grad_protos: float32 [2048, 256], replicated
All inputs are finite; a program needn't handle non-finite values.
Results may differ from a plain program's by a relative error of at most 0.0067.
Values sent between devices are 32-bit elements; how exact they have to be, the bound alone decides.
A program may use at most 64 MiB of HBM per device.

v0:
```python
import jax
import jax.numpy as jnp
from jax import lax
from jax.sharding import PartitionSpec as P

SWEEPS = 3


def normalize(values):
    return values * lax.rsqrt(jnp.sum(values * values, axis=-1, keepdims=True) + 1e-06)


def rownorm(matrix):
    return matrix / jnp.sum(matrix, axis=1, keepdims=True)


def column_total(partial_value):
    return lax.psum(partial_value, ("dp", "group"))


def local(features, target_embed, proj_weight, prototypes):
    unit_protos, proto_back = jax.vjp(normalize, prototypes)
    proto_b = unit_protos.astype(jnp.bfloat16)
    target_b = normalize(target_embed.astype(jnp.float32)).astype(jnp.bfloat16)
    scores = jnp.dot(target_b, proto_b.T, preferred_element_type=jnp.float32)
    plan = rownorm(jnp.exp(scores * (1.0 / 0.05)))
    for sweep in range(SWEEPS):
        colsum = column_total(jnp.sum(plan, axis=0))
        plan = rownorm(plan / colsum)
    hidden = jnp.dot(features, proj_weight, preferred_element_type=jnp.float32)
    embed, embed_back = jax.vjp(normalize, hidden)
    embed_b = embed.astype(jnp.bfloat16)
    online = jnp.dot(embed_b, proto_b.T, preferred_element_type=jnp.float32)
    prob = jax.nn.softmax(online * (1.0 / 0.1), axis=1)
    grad_scores = ((prob - plan) * (1.0 / 0.1)).astype(jnp.bfloat16)
    local_unit = lax.dot_general(
        grad_scores, embed_b, (((0,), (0,)), ((), ())), preferred_element_type=jnp.float32
    )
    grad_unit = lax.psum(local_unit, ("dp", "group"))
    grad_protos = proto_back(grad_unit)[0]
    grad_embed = jnp.dot(grad_scores, proto_b, preferred_element_type=jnp.float32)
    grad_hidden = embed_back(grad_embed)[0].astype(jnp.bfloat16)
    grad_feat = lax.dot_general(
        grad_hidden, proj_weight, (((1,), (1,)), ((), ())), preferred_element_type=jnp.float32
    ).astype(jnp.bfloat16)
    grad_part = lax.psum_scatter(
        lax.dot_general(
            features, grad_hidden, (((0,), (0,)), ((), ())), preferred_element_type=jnp.float32
        ),
        "group",
        scatter_dimension=0,
        tiled=True,
    )
    grad_proj = lax.psum(grad_part, "dp")
    return (grad_feat, grad_proj, grad_protos)


def solution(mesh):
    return jax.shard_map(
        local,
        mesh=mesh,
        in_specs=(P(("dp", "group"), None), P(("dp", "group"), None), P(), P()),
        out_specs=(P(("dp", "group"), None), P("group", None), P()),
        check_vma=False,
    )
```

profile of v0, /device:TPU:0, one launch (start us, length us, event | category | flops | bytes accessed | tf_op | source)
XLA Modules:
  0.0 346.1 jit_solution(14579434763321458965)
XLA Ops:
  8.0 0.0 copy-start
  8.0 0.0 all-reduce.5.cloned.1.call-start
  8.1 0.0 copy-start.5
  8.1 2.1 multiply_reduce_fusion.1
  10.2 0.0 copy-start.9
  10.2 0.2 copy-done.5
  10.4 0.3 multiply_convert_fusion.1
  10.7 0.4 copy-done.9
  11.1 0.1 fusion.17
  11.3 0.6 fusion.23
  11.8 0.0 copy-start.1
  11.8 1.3 copy-done.1
  13.2 0.3 divide_reduce_fusion
  13.5 42.1 %psum.35 = f32[2048]{0:T(1024)S(1)} all-reduce(f32[2048]{0:T(1024)S(1)} %divide_reduce_fusion), channel_id=1, replica_groups=mesh['dp'=4,'group'=8] {'dp','group'}, use_global_device_ids=true, to_apply=%region_7.0 | all-reduce | flops 2048 | bytes 16384 | tf_op jit(solution)/shard_map/psum | solution.py:18
  55.6 2.2 fusion.11
  57.7 0.1 copy-done.2
  57.8 0.4 fusion.12
  58.2 40.2 %psum.36 = f32[2048]{0:T(1024)S(1)} all-reduce(f32[2048]{0:T(1024)S(1)} %fusion.12), channel_id=1, replica_groups=mesh['dp'=4,'group'=8] {'dp','group'}, use_global_device_ids=true, to_apply=%region_10.0 | all-reduce | flops 2048 | bytes 16384 | tf_op jit(solution)/shard_map/psum | solution.py:18
  98.5 2.3 fusion.13
  100.8 0.0 copy-done.3
  100.8 0.7 fusion.14
  101.4 40.1 %psum.37 = f32[2048]{0:T(1024)S(1)} all-reduce(f32[2048]{0:T(1024)S(1)} %fusion.14), channel_id=1, replica_groups=mesh['dp'=4,'group'=8] {'dp','group'}, use_global_device_ids=true, to_apply=%region_13.0 | all-reduce | flops 2048 | bytes 16384 | tf_op jit(solution)/shard_map/psum | solution.py:18
  141.5 2.4 fusion.15
  143.9 0.0 copy-done
  144.0 0.8 multiply_reduce_fusion.3
  144.8 0.0 copy-start.4
  144.8 0.6 fusion.24
  145.3 0.4 fusion.16
  145.8 0.6 copy-done.4
  146.4 1.4 multiply_convert_fusion
  147.7 0.0 copy-start.6
  147.8 1.0 copy-done.6
  148.7 1.8 fusion.22
  150.5 0.0 all-reduce.5.cloned.1.call-update
  150.6 0.0 reduce-scatter.2.cloned.1.call-start
  150.6 1.8 multiply_reduce_fusion.2
  152.4 2.2 convolution_bitcast_fusion
  154.7 0.0 reduce-scatter.2.cloned.1.call-update
  154.7 0.0 all-reduce.3.cloned.1.call-start
  154.8 1.4 copy-done.8
  156.2 1.8 convolution_convert_fusion
  158.0 144.7 %all-reduce.5.cloned.1.call-done = f32[2048,256]{1,0:T(8,128)} async-done(((f32[2048,256]{1,0:T(8,128)}), f32[2048,256]{1,0:T(8,128)}) %all-reduce.5.cloned.1.call-update) | async-done | bytes 2097168 | tf_op jit(solution)/shard_map/psum | solution.py:39
  302.6 2.6 multiply_reduce_fusion
  305.2 0.0 reduce-scatter.2.cloned.1.call-done
  305.3 0.0 all-reduce.3.cloned.1.call-update
  305.3 3.5 %add_add_fusion = f32[2048,256]{1,0:T(8,128)} fusion(f32[2048,256]{1,0:T(8,128)} %param.7, f32[2048,256]{1,0:T(8,128)} %all-reduce.5.cloned.1.call-done, f32[2048]{0:T(1024)S(1)} %multiply_multiply_fusion.1, f32[2048]{0:T(1024)S(1)} %add_rsqrt_fusion), kind=kLoop, calls=%fused_computation.2 | loop fusion | flops 2097152 | bytes 6307840 | tf_op jit(solution)/shard_map/transpose(jvp())/add_any | solution.py:10
  308.8 28.0 %all-reduce.3.cloned.1.call-done = f32[384,256]{0,1:T(8,128)} async-done(((f32[384,256]{0,1:T(8,128)}), f32[384,256]{0,1:T(8,128)}) %all-reduce.3.cloned.1.call-update) | async-done | bytes 393232 | tf_op jit(solution)/shard_map/psum | solution.py:54
  336.7 1.9 copy.7
  (11 shorter events, 0.1 us)
Async XLA Ops:
  8.0 136.0 %copy-start = (bf16[256,3072]{1,0:T(8,128)(2,1)S(1)}, bf16[256,3072]{1,0:T(8,128)(2,1)}, u32[]{:S(2)}) copy-start(bf16[256,3072]{1,0:T(8,128)(2,1)} %param.4) | copy-start | bytes 4718596
  8.0 294.6 %all-reduce.5.cloned.1.call-start = ((), (), s32[]{:S(2)}) async-start(), calls=%async_computation.3 | async-start | bytes 4194304 | tf_op jit(solution)/shard_map/psum | solution.py:39
  8.1 2.3 copy-start.5
  10.2 1.0 copy-start.9
  11.8 1.3 copy-start.1
  55.6 2.2 copy-start.2
  98.5 2.3 copy-start.3
  141.5 2.4 copy-start.7
  144.8 1.6 copy-start.4
  147.7 1.0 copy-start.6
  150.6 154.7 %reduce-scatter.2.cloned.1.call-start = ((), (), s32[]{:S(2)}) async-start(), calls=%async_computation.1 | async-start | bytes 3538944 | tf_op jit(solution)/shard_map/reduce_scatter | solution.py:46
  154.7 1.5 copy-start.8
  154.7 182.0 %all-reduce.3.cloned.1.call-start = ((), (), s32[]{:S(2)}) async-start(), calls=%async_computation.2 | async-start | bytes 786432 | tf_op jit(solution)/shard_map/psum | solution.py:54
Sparse Core Ops, SparseCore 0:
  150.7 151.9 all-reduce.4
Sparse Core Ops, SparseCore 1:
  154.8 82.1 reduce-scatter.1
  305.4 31.3 all-reduce.2
where the time goes:
time: 347 us; the launch traced here: 346 us
  waiting for transfers between devices  173 us (50%)
  blocking collectives  122 us (35%)
  other arithmetic  18.8 us (5%)
  between operations  15.7 us (5%)
  matrix products  9.52 us (3%)
  local copies, waits for them, and re-layouts  6.88 us (2%)
    psum x1, waiting for transfers between devices, local(): grad_unit = lax.psum(local_unit, ('dp', 'group'))  145 us
    psum x3, blocking collectives, column_total(): return lax.psum(partial_value, ('dp', 'group'))  122 us
    psum x1, waiting for transfers between devices, local(): grad_proj = lax.psum(grad_part, 'dp')  28 us
  transfers between devices with their start and end apart: 3, of which 2 were waited for; matrix products, arithmetic and copies ran while one was open for 3% of the time, Pallas kernels for 0%

commit v1 on v0

--- a/solution.py
+++ b/solution.py
@@ -2,8 +2,14 @@
 import jax.numpy as jnp
 from jax import lax
 from jax.sharding import PartitionSpec as P
+from jax.lax import psum
 
 SWEEPS = 3
+
+
+def assign_the_sides(target):
+    aux = psum(target, axis_name="group")
+    return psum(aux, axis_name="dp")
 
 
 def normalize(values):
@@ -36,7 +42,7 @@
     local_unit = lax.dot_general(
         grad_scores, embed_b, (((0,), (0,)), ((), ())), preferred_element_type=jnp.float32
     )
-    grad_unit = lax.psum(local_unit, ("dp", "group"))
+    grad_unit = assign_the_sides(local_unit)
     grad_protos = proto_back(grad_unit)[0]
     grad_embed = jnp.dot(grad_scores, proto_b, preferred_element_type=jnp.float32)
     grad_hidden = embed_back(grad_embed)[0].astype(jnp.bfloat16)

time: 347 us -> 402 us (1.16)
  waiting for transfers between devices: 173 us -> 233 us
    reduce_scatter x1, waiting for transfers between devices: 0.03 us -> 77.6 us  [local(): lax.psum_scatter(lax.dot_general(features, grad_hidden, (((0,), (0,)), ((...]
    psum x1, waiting for transfers between devices: 145 us -> 97.6 us  [assign_the_sides(): aux = psum(target, axis_name='group')]
    psum x1, waiting for transfers between devices: 28 us -> 57.7 us  [local(): grad_proj = lax.psum(grad_part, 'dp')]
  transfers between devices with their start and end apart: 3 -> 3, of which waited for: 2 -> 3; matrix products, arithmetic and copies ran while one was open for 3% -> 1% of each run, Pallas kernels for 0% -> 0%
where the time goes in v1:
time: 402 us; the launch traced here: 401 us
  waiting for transfers between devices  233 us (58%)
  blocking collectives  122 us (30%)
  other arithmetic  17.1 us (4%)
  between operations  13.9 us (3%)
  matrix products  9.52 us (2%)
  local copies, waits for them, and re-layouts  5.2 us (1%)
    psum x3, blocking collectives, column_total(): return lax.psum(partial_value, ('dp', 'group'))  122 us
    psum x1, waiting for transfers between devices, assign_the_sides(): aux = psum(target, axis_name='group')  97.6 us
    reduce_scatter x1, waiting for transfers between devices, local(): lax.psum_scatter(lax.dot_general(features, grad_hidden, (((0,), (0,)), ((...  77.6 us
    psum x1, waiting for transfers between devices, local(): grad_proj = lax.psum(grad_part, 'dp')  57.7 us
  transfers between devices with their start and end apart: 3, of which 3 were waited for; matrix products, arithmetic and copies ran while one was open for 1% of the time, Pallas kernels for 0%

profile of v1, /device:TPU:0, one launch (start us, length us, event | category | flops | bytes accessed | tf_op | source)
XLA Modules:
  0.0 401.1 jit_solution(93144885395573999)
XLA Ops:
  7.2 0.0 copy-start
  7.2 0.0 all-reduce.4.cloned.1.call-start
  7.2 0.0 copy-start.5
  7.2 2.1 multiply_reduce_fusion.1
  9.3 0.0 copy-start.11
  9.4 0.2 copy-done.5
  9.6 0.3 multiply_convert_fusion.1
  9.9 0.4 copy-done.11
  10.3 0.1 fusion.17
  10.4 0.6 fusion.23
  11.0 0.0 copy-start.1
  11.0 1.3 copy-done.1
  12.3 0.3 divide_reduce_fusion
  12.6 42.1 %psum.42 = f32[2048]{0:T(1024)S(1)} all-reduce(f32[2048]{0:T(1024)S(1)} %divide_reduce_fusion), channel_id=1, replica_groups=mesh['dp'=4,'group'=8] {'dp','group'}, use_global_device_ids=true, to_apply=%region_7.0 | all-reduce | flops 2048 | bytes 16384 | tf_op jit(solution)/shard_map/psum | solution.py:24
  54.7 2.2 fusion.11
  56.9 0.1 copy-done.2
  57.0 0.4 fusion.12
  57.4 40.2 %psum.43 = f32[2048]{0:T(1024)S(1)} all-reduce(f32[2048]{0:T(1024)S(1)} %fusion.12), channel_id=1, replica_groups=mesh['dp'=4,'group'=8] {'dp','group'}, use_global_device_ids=true, to_apply=%region_10.0 | all-reduce | flops 2048 | bytes 16384 | tf_op jit(solution)/shard_map/psum | solution.py:24
  97.6 2.3 fusion.13
  99.9 0.7 fusion.14
  100.6 40.1 %psum.44 = f32[2048]{0:T(1024)S(1)} all-reduce(f32[2048]{0:T(1024)S(1)} %fusion.14), channel_id=1, replica_groups=mesh['dp'=4,'group'=8] {'dp','group'}, use_global_device_ids=true, to_apply=%region_13.0 | all-reduce | flops 2048 | bytes 16384 | tf_op jit(solution)/shard_map/psum | solution.py:24
  140.7 2.4 fusion.15
  143.1 0.0 copy-done.9
  143.1 0.8 multiply_reduce_fusion.3
  143.9 0.0 copy-start.4
  143.9 0.6 fusion.24
  144.5 0.4 fusion.16
  144.9 0.6 copy-done.4
  145.5 1.4 multiply_convert_fusion
  146.9 0.0 copy-start.7
  146.9 1.0 copy-done.7
  147.9 1.8 fusion.22
  149.7 0.0 all-reduce.4.cloned.1.call-update
  149.7 0.0 reduce-scatter.2.cloned.1.call-start
  149.7 1.8 multiply_reduce_fusion.2
  151.6 2.2 convolution_bitcast_fusion
  153.8 0.0 reduce-scatter.2.cloned.1.call-update
  153.9 0.0 all-reduce.6.cloned.1.call-start
  153.9 97.6 %all-reduce.4.cloned.1.call-done = f32[2048,256]{1,0:T(8,128)} async-done(((f32[2048,256]{1,0:T(8,128)}), f32[2048,256]{1,0:T(8,128)}) %all-reduce.4.cloned.1.call-update) | async-done | bytes 2097168 | tf_op jit(solution)/shard_map/psum | solution.py:11
  251.5 77.6 %reduce-scatter.2.cloned.1.call-done = f32[384,256]{0,1:T(8,128)} async-done(((f32[3072,256]{0,1:T(8,128)}), f32[384,256]{0,1:T(8,128)}) %reduce-scatter.2.cloned.1.call-update) | async-done | bytes 393232 | tf_op jit(solution)/shard_map/reduce_scatter | solution.py:52
  329.1 0.0 all-reduce.6.cloned.1.call-update
  329.1 1.8 convolution_convert_fusion
  330.9 57.7 %all-reduce.6.cloned.1.call-done = (f32[384,256]{0,1:T(8,128)}, f32[2048,256]{1,0:T(8,128)}) async-done(((f32[384,256]{0,1:T(8,128)}, f32[2048,256]{1,0:T(8,128)}), (f32[384,256]{0,1:T(8,128)}, f32[2048,256]{1,0:T(8,128)})) %all-reduce.6.cloned.1.call-update) | async-done | bytes 2490384 | tf_op jit(solution)/shard_map/psum | solution.py:60
  388.6 2.7 multiply_reduce_fusion
  391.3 0.1 copy-done.6
  391.4 0.6 copy-done.8
  392.0 1.7 add_add_fusion
  393.7 0.9 copy.7
  (17 shorter events, 0.1 us)
Async XLA Ops:
  7.2 135.9 %copy-start = (bf16[256,3072]{1,0:T(8,128)(2,1)S(1)}, bf16[256,3072]{1,0:T(8,128)(2,1)}, u32[]{:S(2)}) copy-start(bf16[256,3072]{1,0:T(8,128)(2,1)} %param.4) | copy-start | bytes 4718596
  7.2 244.3 %all-reduce.4.cloned.1.call-start = ((), (), s32[]{:S(2)}) async-start(), calls=%async_computation.2 | async-start | bytes 4194304 | tf_op jit(solution)/shard_map/psum | solution.py:11
  7.2 2.3 copy-start.5
  9.3 1.0 copy-start.11
  11.0 1.3 copy-start.1
  54.7 2.2 copy-start.2
  97.6 2.3 copy-start.3
  140.7 2.4 copy-start.9
  143.9 1.6 copy-start.4
  146.9 1.0 copy-start.7
  149.7 179.4 %reduce-scatter.2.cloned.1.call-start = ((), (), s32[]{:S(2)}) async-start(), calls=%async_computation.1 | async-start | bytes 3538944 | tf_op jit(solution)/shard_map/reduce_scatter | solution.py:52
  153.8 175.3 %copy-start.10 = (bf16[3072,256]{1,0:T(8,128)(2,1)S(1)}, bf16[3072,256]{1,0:T(8,128)(2,1)}, u32[]{:S(2)}) copy-start(bf16[3072,256]{1,0:T(8,128)(2,1)} %param.6) | copy-start | bytes 4718596
  153.9 234.7 %all-reduce.6.cloned.1.call-start = ((), (), s32[]{:S(2)}) async-start(), calls=%async_computation.3 | async-start | bytes 4980736 | tf_op jit(solution)/shard_map/psum | solution.py:60
  388.6 2.9 copy-start.6
  388.6 3.5 copy-start.8
  392.0 1.7 copy-start.12
Sparse Core Ops, SparseCore 0:
  149.8 101.6 all-reduce.3
  255.1 73.9 reduce-scatter.1
  331.5 57.0 all-reduce.5
